TPU v7x, 32 devices: a whole 2x2x4 slice. The times are simulated.
32 devices in a mesh: groups: 2 (over y), seg: 4 (over z), ch: 2 (over x), sub: 2 (over core).
Axes of the slice: x: 2, y: 2, z: 4, core: 2. Of those that a mesh axis runs over, the one named last changes fastest.
Arguments:
- rank_series: bfloat16 [2048, 16384], P(('groups', 'ch', 'sub'), 'seg'), parts along dimension 0, may hold values from -6 to 6
- power_series: bfloat16 [2048, 16384], P(('groups', 'ch', 'sub'), 'seg'), parts along dimension 0, may hold values from -6 to 6
- seg_offsets: int32 [32], P(('groups', 'seg')), parts along dimension 0, may hold values from 2048 to 4095, as said below
- bin_index: int32 [128], replicated, may hold values from 0 to 511, as said below
Outputs:
- cross_spectra: bfloat16 [2, 256, 1024, 1024], P(None, ('groups', 'seg'), ('ch', 'sub')), parts along dimension 1
There are 2 independent parts, one for each index of `groups`. A program takes and returns all parts, laid end to end along the dimension named above; an argument that names none is the same for every part. Nothing has to cross between parts.
Inputs may be any that keep to these rules, and one draw needn't show every extreme that they name: `seg_offsets`: every segment reads at least half of its samples past its own 4096 samples, in the following ones. `bin_index`: the bins are distinct.
All inputs are finite; a program needn't handle non-finite values.
Results may differ from a plain program's by a relative error of at most 0.0055.
Values may be sent and summed in bfloat16 or wider, within the bound.
A program may use at most 192 MiB of HBM per device.

v0:
```python
import math
import jax
import jax.numpy as jnp
from jax import lax
from jax.sharding import PartitionSpec as P


def shifted(array, axis, by):
    peers = lax.axis_size(axis)
    pairs = [(i, i + by) for i in range(peers) if 0 <= i + by < peers]
    return lax.ppermute(array, axis, pairs)


def make_kernel(bin_index, length):
    sample_ids = jnp.arange(length, dtype=jnp.int32)
    window = 0.5 - 0.5 * jnp.cos(2.0 * math.pi / length * sample_ids.astype(jnp.float32))
    phase = bin_index[:, None] * sample_ids[None, :] % length
    angle = 2.0 * math.pi / length * phase.astype(jnp.float32)
    factor = (3.0 * length / 8.0) ** (-0.5)
    waves = jnp.stack([jnp.cos(angle), -jnp.sin(angle)]) * factor
    return (waves * window).astype(jnp.bfloat16)


def cut_segments(extended, offsets, length):

    def one_segment(offset):
        return lax.dynamic_slice_in_dim(extended, offset, length, 1)

    return jax.vmap(one_segment)(offsets)


def transform(segments, kernel):
    return jnp.einsum("tkn,scn->stkc", kernel, segments, preferred_element_type=jnp.float32)


def body(rank_series, power_series, seg_offsets, bin_index):
    length = rank_series.shape[1]
    rank_width = rank_series.shape[0]
    series_all = jnp.concatenate([rank_series, power_series], axis=0)
    kernel = make_kernel(bin_index, length)
    next_rim = shifted(series_all, "seg", -1)
    extended = jnp.concatenate([series_all, next_rim], axis=1)
    spectra = transform(cut_segments(extended, seg_offsets, length), kernel)
    spectra = spectra.astype(jnp.bfloat16)
    owned = lax.all_to_all(spectra, "seg", split_axis=2, concat_axis=0, tiled=True)
    rank_owned = owned[..., :rank_width]
    power_owned = owned[..., rank_width:]
    power_piece = lax.all_gather(power_owned, ("ch", "sub"), axis=3, tiled=True)
    swapped = jnp.concatenate([power_piece[:, 1:2], -power_piece[:, 0:1]], axis=1)
    real_part = jnp.einsum(
        "gtkr,gtkp->krp", rank_owned, power_piece, preferred_element_type=jnp.float32
    )
    imag_part = jnp.einsum(
        "gtkr,gtkp->krp", rank_owned, swapped, preferred_element_type=jnp.float32
    )
    return jnp.stack([real_part, imag_part]).astype(jnp.bfloat16)


def solution(mesh):
    return jax.shard_map(
        body,
        mesh=mesh,
        in_specs=(
            P(("groups", "ch", "sub"), "seg"),
            P(("groups", "ch", "sub"), "seg"),
            P(("groups", "seg")),
            P(),
        ),
        out_specs=P(None, ("groups", "seg"), ("ch", "sub"), None),
        check_vma=False,
    )
```

profile of v0, /device:TPU:0, one launch (start us, length us, event | category | flops | bytes accessed | tf_op | source)
XLA Modules:
  0.0 261.1 jit_solution(1151138796967690156)
XLA Ops:
  6.5 0.0 copy-start.1
  6.5 0.0 copy-start.3
  6.5 0.0 copy-start.2
  6.5 0.0 all-gather.2.cloned.1.call-start
  6.5 3.3 %constant_dynamic-update-slice_fusion.1 = bf16[512,4096]{1,0:T(8,128)(2,1)} fusion(bf16[256,4096]{1,0:T(8,128)(2,1)} %param.4), kind=kLoop, calls=%fused_computation.35 | loop fusion | bytes 4194304
  9.8 0.0 copy-done.1
  9.8 1.4 constant_dynamic-update-slice_fusion
  11.3 1.3 collective-permute-start
  12.6 0.0 copy-done.3
  12.6 0.1 subtract_multiply_fusion
  12.7 0.0 copy-done.2
  12.7 9.7 %fusion.27 = (f32[1,128,4096]{2,1,0:T(8,128)S(1)}, f32[1,128,4096]{2,1,0:T(8,128)}) fusion(s32[128]{0:T(128)S(1)} %copy-done.2), kind=kLoop, calls=%fused_computation.30 | loop fusion | flops 7864320 | bytes 4194816 | tf_op jit(solution)/shard_map/cos | solution.py:20
  22.4 84.7 %collective-permute-done = bf16[512,4096]{1,0:T(8,128)(2,1)} collective-permute-done((bf16[512,4096]{1,0:T(8,128)(2,1)}, bf16[512,4096]{1,0:T(8,128)(2,1)}, u32[]{:S(2)}, u32[]{:S(2)}) %collective-permute-start) | collective-permute-done | bytes 4194336 | tf_op jit(solution)/shard_map/ppermute | solution.py:11
  107.1 7.7 %pad_maximum_fusion.1 = bf16[512,8192]{1,0:T(8,128)(2,1)} fusion(bf16[512,4096]{1,0:T(8,128)(2,1)} %collective-permute-done, bf16[512,4096]{1,0:T(8,128)(2,1)} %constant_dynamic-update-slice_fusion), kind=kLoop, calls=%fused_computation.9 | loop fusion | flops 16777216 | bytes 16777216 | tf_op jit(solution)/shard_map/concatenate | solution.py:42
  114.8 32.7 %while.1 = (s32[]{:T(128)}, bf16[512,8192]{1,0:T(8,128)(2,1)}, s32[4,2]{0,1:T(2,128)S(1)}, bf16[4,512,4096]{2,1,0:T(8,128)(2,1)}, s32[]{:T(128)}) while((s32[]{:T(128)}, bf16[512,8192]{1,0:T(8,128)(2,1)}, s32[4,2]{0,1:T(2,128)S(1)}, bf16[4,512,4096]{2,1,0:T(8,128)(2,1)}, s32[]{:T(128)}) %tuple.18), condition=%wide.while_cond, body=%wide.while_body.sunk | while | flops 2 | bytes 8389221 | solution.py:27
  114.8 0.1 constant_dynamic-slice_fusion.2
  114.8 0.6 slice.38
  115.4 7.5 %bitcast_dynamic-update-slice_fusion.2 = bf16[4,512,4096]{2,1,0:T(8,128)(2,1)} fusion(bf16[4,512,4096]{2,1,0:T(8,128)(2,1)} %get-tuple-element.58, s32[]{:T(128)S(6)} %copy.18, bf16[512,8192]{1,0:T(8,128)(2,1)} %get-tuple-element.61, s32[]{:T(128)} %bitcast.46), kind=kLoop, calls=%fused_computation.clone.1 | loop fusion | bytes 8389124 | tf_op jit(solution)/shard_map/vmap()/gather
  122.9 0.1 constant_dynamic-slice_fusion.2
  123.0 0.6 slice.38
  123.6 7.5 %bitcast_dynamic-update-slice_fusion.2 = bf16[4,512,4096]{2,1,0:T(8,128)(2,1)} fusion(bf16[4,512,4096]{2,1,0:T(8,128)(2,1)} %get-tuple-element.58, s32[]{:T(128)S(6)} %copy.18, bf16[512,8192]{1,0:T(8,128)(2,1)} %get-tuple-element.61, s32[]{:T(128)} %bitcast.46), kind=kLoop, calls=%fused_computation.clone.1 | loop fusion | bytes 8389124 | tf_op jit(solution)/shard_map/vmap()/gather
  131.1 0.1 constant_dynamic-slice_fusion.2
  131.2 0.6 slice.38
  131.8 7.5 %bitcast_dynamic-update-slice_fusion.2 = bf16[4,512,4096]{2,1,0:T(8,128)(2,1)} fusion(bf16[4,512,4096]{2,1,0:T(8,128)(2,1)} %get-tuple-element.58, s32[]{:T(128)S(6)} %copy.18, bf16[512,8192]{1,0:T(8,128)(2,1)} %get-tuple-element.61, s32[]{:T(128)} %bitcast.46), kind=kLoop, calls=%fused_computation.clone.1 | loop fusion | bytes 8389124 | tf_op jit(solution)/shard_map/vmap()/gather
  139.3 0.1 constant_dynamic-slice_fusion.2
  139.4 0.6 slice.38
  139.9 7.5 %bitcast_dynamic-update-slice_fusion.2 = bf16[4,512,4096]{2,1,0:T(8,128)(2,1)} fusion(bf16[4,512,4096]{2,1,0:T(8,128)(2,1)} %get-tuple-element.58, s32[]{:T(128)S(6)} %copy.18, bf16[512,8192]{1,0:T(8,128)(2,1)} %get-tuple-element.61, s32[]{:T(128)} %bitcast.46), kind=kLoop, calls=%fused_computation.clone.1 | loop fusion | bytes 8389124 | tf_op jit(solution)/shard_map/vmap()/gather
  147.5 8.8 %fusion.22 = bf16[4,2,128,512]{2,3,1,0:T(8,128)(2,1)S(1)} fusion(f32[1,128,4096]{2,1,0:T(8,128)} %get-tuple-element.24, f32[1,128,4096]{2,1,0:T(8,128)S(1)} %get-tuple-element.23, f32[4096]{0:T(1024)S(1)} %subtract_multiply_fusion, bf16[4,512,4096]{2,1,0:T(8,128)(2,1)} %get-tuple-element.12), kind=kOutput, calls=%fused_computation.28 | convolution fusion | flops 4298637312 | bytes 22036480 | tf_op jit(solution)/shard_map/tkn,scn->stkc/dot_general | solution.py:33
  156.3 1.0 copy.8
  157.2 28.7 %all_to_all.18 = bf16[4,2,128,512]{3,1,0,2:T(2,128)(2,1)S(1)} all-to-all(bf16[4,2,128,512]{3,1,0,2:T(2,128)(2,1)S(1)} %copy.8), channel_id=1, replica_groups=mesh['groups'=2,'seg'=4,'ch'=2,'sub'=2] {'seg'}, dimensions={2} | all-to-all | bytes 2097152 | tf_op jit(solution)/shard_map/all_to_all | solution.py:45
  185.9 0.3 copy.9
  186.2 0.8 copy.10
  187.1 0.3 all_to_all.16
  187.3 0.8 slice.28
  188.2 0.0 all-gather.2.cloned.1.call-update
  188.2 22.1 %all-gather.2.cloned.1.call-done = bf16[16,2,32,1024]{3,0,1,2:T(8,128)(2,1)} async-done(((bf16[16,2,32,256]{3,0,1,2:T(8,128)(2,1)}), bf16[16,2,32,1024]{3,0,1,2:T(8,128)(2,1)}) %all-gather.2.cloned.1.call-update) | async-done | bytes 2097168 | tf_op jit(solution)/shard_map/all_gather | solution.py:48
  210.3 3.0 %fusion.33 = (bf16[16,1,32,1024]{3,0,1,2:T(8,128)(2,1)}, bf16[16,1,32,1024]{3,0,1,2:T(8,128)(2,1)}) fusion(bf16[16,2,32,1024]{3,0,1,2:T(8,128)(2,1)} %all-gather.2.cloned.1.call-done), kind=kLoop, calls=%fused_computation.40 | loop fusion | flops 524288 | bytes 4194304 | tf_op jit(solution)/shard_map/slice | solution.py:49
  213.3 0.0 copy-start
  213.3 9.8 %fusion.1 = bf16[1,32,256,1024]{3,2,1,0:T(8,128)(2,1)} fusion(bf16[16,1,32,1024]{3,0,1,2:T(8,128)(2,1)} %get-tuple-element.22, bf16[16,1,32,1024]{3,0,1,2:T(8,128)(2,1)} %get-tuple-element.21, bf16[16,2,32,512]{3,0,1,2:T(8,128)(2,1)S(1)} %all_to_all.16), kind=kOutput, calls=%fused_computation.6 | convolution fusion | flops 546308096 | bytes 19398656 | tf_op jit(solution)/shard_map/gtkr,gtkp->krp/dot_general | solution.py:53
  223.1 0.0 copy-done
  223.1 8.1 %fusion = bf16[1,32,256,1024]{3,2,1,0:T(8,128)(2,1)} fusion(bf16[16,2,32,1024]{3,0,1,2:T(8,128)(2,1)S(1)} %copy-done, bf16[16,2,32,512]{3,0,1,2:T(8,128)(2,1)S(1)} %all_to_all.16), kind=kOutput, calls=%fused_computation.5 | convolution fusion | flops 545259520 | bytes 19398656 | tf_op jit(solution)/shard_map/gtkr,gtkp->krp/dot_general | solution.py:50
  231.2 23.0 %pad_maximum_fusion = bf16[2,32,256,1024]{3,2,1,0:T(8,128)(2,1)} fusion(bf16[1,32,256,1024]{3,2,1,0:T(8,128)(2,1)} %fusion.1, bf16[1,32,256,1024]{3,2,1,0:T(8,128)(2,1)} %fusion), kind=kLoop, calls=%fused_computation.2 | loop fusion | flops 16777216 | bytes 67108864 | tf_op jit(solution)/shard_map/stack | solution.py:56
  (3 shorter events, 0.0 us)
Async XLA Ops:
  6.5 3.3 %copy-start.1 = (bf16[256,4096]{1,0:T(8,128)(2,1)S(1)}, bf16[256,4096]{1,0:T(8,128)(2,1)}, u32[]{:S(2)}) copy-start(bf16[256,4096]{1,0:T(8,128)(2,1)} %param.5) | copy-start | bytes 6291460
  6.5 6.0 %copy-start.3 = (s32[4]{0:T(128)S(1)}, s32[4]{0:T(128)}, u32[]{:S(2)}) copy-start(s32[4]{0:T(128)} %param.6) | copy-start | bytes 52
  6.5 6.1 %copy-start.2 = (s32[128]{0:T(128)S(1)}, s32[128]{0:T(128)}, u32[]{:S(2)}) copy-start(s32[128]{0:T(128)} %param.7) | copy-start | bytes 1540
  6.5 203.8 %all-gather.2.cloned.1.call-start = ((), (), s32[]{:S(2)}) async-start(), calls=%async_computation.1 | async-start | bytes 2621440 | tf_op jit(solution)/shard_map/all_gather | solution.py:48
  11.3 95.8 %collective-permute-start = (bf16[512,4096]{1,0:T(8,128)(2,1)}, bf16[512,4096]{1,0:T(8,128)(2,1)}, u32[]{:S(2)}, u32[]{:S(2)}) collective-permute-start(bf16[512,4096]{1,0:T(8,128)(2,1)} %constant_dynamic-update-slice_fusion), channel_id=1, source_target_pairs={{4,0},{8,4},{12,8},{5,1},{9,5},{13,9},{6,2},{10,6},{14,10},{7,3},{... | collective-permute-start | bytes 12582920 | tf_op jit(solution)/shard_map/ppermute | solution.py:11
  213.3 9.8 %copy-start = (bf16[16,2,32,1024]{3,0,1,2:T(8,128)(2,1)S(1)}, bf16[16,2,32,1024]{3,0,1,2:T(8,128)(2,1)}, u32[]{:S(2)}) copy-start(bf16[16,2,32,1024]{3,0,1,2:T(8,128)(2,1)} %all-gather.2.cloned.1.call-done) | copy-start | bytes 6291460
Sparse Core Ops, SparseCore 0:
  188.3 21.9 all-gather.1
where the time goes:
time: 261 us
  waiting for transfers between devices  107 us (41%)
  other arithmetic  43.4 us (17%)
  local copies, waits for them, and re-layouts  40.7 us (16%)
  blocking collectives  28.7 us (11%)
  matrix products  26.7 us (10%)
  between operations  13.5 us (5%)
    ppermute x1, waiting for transfers between devices, shifted(): return lax.ppermute(array, axis, pairs)  84.7 us
    gather x12, local copies, waits for them, and re-layouts  32.7 us
    all_to_all x1, blocking collectives, body(): lax.all_to_all(spectra, 'seg', split_axis=2, concat_axis=0, tiled=True)  28.7 us
    another operation x1, other arithmetic, body(): return jnp.stack([real_part, imag_part]).astype(jnp.bfloat16)  23 us
    all_gather x1, waiting for transfers between devices, body(): power_piece = lax.all_gather(power_owned, ('ch', 'sub'), axis=3, tiled=True)  22.1 us
    dot_general x1, matrix products, body(): jnp.einsum('gtkr,gtkp->krp', rank_owned, swapped, preferred_element_type=...  9.81 us
    cos x1, other arithmetic, make_kernel(): waves = jnp.stack([jnp.cos(angle), -jnp.sin(angle)]) * factor  9.69 us
    dot_general x1, matrix products, transform(): jnp.einsum('tkn,scn->stkc', kernel, segments, preferred_element_type=jnp....  8.77 us
  transfers between devices with their start and end apart: 2, of which 2 were waited for; matrix products, arithmetic and copies ran while one was open for 4% of the time, Pallas kernels for 0%

commit v1 on v0

--- a/solution.py
+++ b/solution.py
@@ -3,6 +3,24 @@
 import jax.numpy as jnp
 from jax import lax
 from jax.sharding import PartitionSpec as P
+
+
+def gather_around(shard, axis, dim):
+    ways, here, lap = (lax.axis_size(axis), lax.axis_index(axis), shard.shape[dim])
+    lengths = [n * ways if d == dim else n for d, n in enumerate(shard.shape)]
+    full = lax.dynamic_update_slice_in_dim(
+        jnp.zeros(lengths, shard.dtype), shard, here * lap, axis=dim
+    )
+    going_up = going_down = shard
+    for far in range(1, ways // 2 + 1):
+        going_up = lax.ppermute(going_up, axis, [(d, (d + 1) % ways) for d in range(ways)])
+        full = lax.dynamic_update_slice_in_dim(full, going_up, (here - far) % ways * lap, axis=dim)
+        if 2 * far < ways:
+            going_down = lax.ppermute(going_down, axis, [(d, (d - 1) % ways) for d in range(ways)])
+            full = lax.dynamic_update_slice_in_dim(
+                full, going_down, (here + far) % ways * lap, axis=dim
+            )
+    return full
 
 
 def shifted(array, axis, by):
@@ -45,7 +63,7 @@
     owned = lax.all_to_all(spectra, "seg", split_axis=2, concat_axis=0, tiled=True)
     rank_owned = owned[..., :rank_width]
     power_owned = owned[..., rank_width:]
-    power_piece = lax.all_gather(power_owned, ("ch", "sub"), axis=3, tiled=True)
+    power_piece = gather_around(power_owned, ("ch", "sub"), 3)
     swapped = jnp.concatenate([power_piece[:, 1:2], -power_piece[:, 0:1]], axis=1)
     real_part = jnp.einsum(
         "gtkr,gtkp->krp", rank_owned, power_piece, preferred_element_type=jnp.float32

time: 261 us -> 249 us (0.954)
  blocking collectives: 28.7 us -> 0 us
  waiting for transfers between devices: 107 us -> 127 us
  between operations: 13.5 us -> 0.28 us
  starting transfers between devices: 1.28 us -> 7.04 us
  local copies, waits for them, and re-layouts: 40.7 us -> 45.7 us
    all_to_all x1 -> x0, blocking collectives: 28.7 us -> none  [body(): lax.all_to_all(spectra, 'seg', split_axis=2, concat_axis=0, tiled=True)]
    all_to_all x0 -> x1, waiting for transfers between devices: none -> 24.9 us  [body(): lax.all_to_all(spectra, 'seg', split_axis=2, concat_axis=0, tiled=True)]
    all_gather x1 -> x0, waiting for transfers between devices: 22.1 us -> none  [body(): power_piece = lax.all_gather(power_owned, ('ch', 'sub'), axis=3, tiled=True)]
    ppermute x0 -> x3, waiting for transfers between devices: none -> 17.7 us  [the longest x2 17.7 us: gather_around(): lax.ppermute(going_up, axis, [(d, (d + 1) % ways) for d in range(ways)])]
    all_to_all x0 -> x1, starting transfers between devices: none -> 4.01 us  [body(): lax.all_to_all(spectra, 'seg', split_axis=2, concat_axis=0, tiled=True)]
    dynamic_update_slice x0 -> x3, local copies, waits for them, and re-layouts: none -> 3.31 us  [the longest x2 2.2 us: gather_around(): lax.dynamic_update_slice_in_dim(full, going_up, (here - far) % ways * lap...]
  transfers between devices with their start and end apart: 2 -> 5, of which waited for: 2 -> 4; matrix products, arithmetic and copies ran while one was open for 4% -> 5% of each run, Pallas kernels for 0% -> 0%
where the time goes in v1:
time: 249 us
  waiting for transfers between devices  127 us (51%)
  local copies, waits for them, and re-layouts  45.7 us (18%)
  other arithmetic  41.9 us (17%)
  matrix products  26.5 us (11%)
  starting transfers between devices  7.04 us (3%)
    ppermute x1, waiting for transfers between devices, shifted(): return lax.ppermute(array, axis, pairs)  84.7 us
    gather x12, local copies, waits for them, and re-layouts  33.1 us
    all_to_all x1, waiting for transfers between devices, body(): lax.all_to_all(spectra, 'seg', split_axis=2, concat_axis=0, tiled=True)  24.9 us
    another operation x1, other arithmetic, body(): return jnp.stack([real_part, imag_part]).astype(jnp.bfloat16)  23 us
    ppermute x2, waiting for transfers between devices, gather_around(): lax.ppermute(going_up, axis, [(d, (d + 1) % ways) for d in range(ways)])  17.7 us
    cos x1, other arithmetic, make_kernel(): waves = jnp.stack([jnp.cos(angle), -jnp.sin(angle)]) * factor  9.7 us
    dot_general x1, matrix products, body(): jnp.einsum('gtkr,gtkp->krp', rank_owned, swapped, preferred_element_type=...  9.63 us
    dot_general x1, matrix products, transform(): jnp.einsum('tkn,scn->stkc', kernel, segments, preferred_element_type=jnp....  8.77 us
  transfers between devices with their start and end apart: 5, of which 4 were waited for; matrix products, arithmetic and copies ran while one was open for 5% of the time, Pallas kernels for 0%

profile of v1, /device:TPU:0, one launch (start us, length us, event | category | flops | bytes accessed | tf_op | source)
XLA Modules:
  0.0 248.7 jit_solution(6503965116900691739)
XLA Ops:
  0.0 0.0 copy-start
  0.0 3.3 %constant_dynamic-update-slice_fusion.1 = bf16[512,4096]{1,0:T(8,128)(2,1)} fusion(bf16[256,4096]{1,0:T(8,128)(2,1)} %param.4), kind=kLoop, calls=%fused_computation.35 | loop fusion | bytes 4194304
  3.3 0.0 copy-done
  3.3 0.0 copy-start.2
  3.3 0.0 copy-start.1
  3.3 1.4 constant_dynamic-update-slice_fusion
  4.7 1.3 collective-permute-start
  6.0 0.0 copy-done.2
  6.0 0.1 subtract_multiply_fusion
  6.1 0.0 copy-done.1
  6.1 9.7 %fusion.27 = (f32[1,128,4096]{2,1,0:T(8,128)S(1)}, f32[1,128,4096]{2,1,0:T(8,128)}) fusion(s32[128]{0:T(128)S(1)} %copy-done.1), kind=kLoop, calls=%fused_computation.30 | loop fusion | flops 7864320 | bytes 4194816 | tf_op jit(solution)/shard_map/cos | solution.py:38
  15.8 84.7 %collective-permute-done = bf16[512,4096]{1,0:T(8,128)(2,1)} collective-permute-done((bf16[512,4096]{1,0:T(8,128)(2,1)}, bf16[512,4096]{1,0:T(8,128)(2,1)}, u32[]{:S(2)}, u32[]{:S(2)}) %collective-permute-start) | collective-permute-done | bytes 4194336 | tf_op jit(solution)/shard_map/ppermute | solution.py:29
  100.5 7.7 %pad_maximum_fusion.1 = bf16[512,8192]{1,0:T(8,128)(2,1)} fusion(bf16[512,4096]{1,0:T(8,128)(2,1)} %collective-permute-done, bf16[512,4096]{1,0:T(8,128)(2,1)} %constant_dynamic-update-slice_fusion), kind=kLoop, calls=%fused_computation.9 | loop fusion | flops 16777216 | bytes 16777216 | tf_op jit(solution)/shard_map/concatenate | solution.py:60
  108.2 33.1 %while.1 = (s32[]{:T(128)}, bf16[512,8192]{1,0:T(8,128)(2,1)}, s32[4,2]{0,1:T(2,128)S(1)}, bf16[4,512,4096]{2,1,0:T(8,128)(2,1)}, s32[]{:T(128)}) while((s32[]{:T(128)}, bf16[512,8192]{1,0:T(8,128)(2,1)}, s32[4,2]{0,1:T(2,128)S(1)}, bf16[4,512,4096]{2,1,0:T(8,128)(2,1)}, s32[]{:T(128)}) %tuple.19), condition=%wide.while_cond, body=%wide.while_body.sunk | while | flops 2 | bytes 8389221 | solution.py:45
  108.2 0.1 constant_dynamic-slice_fusion.2
  108.3 0.6 slice.40
  108.9 7.6 %bitcast_dynamic-update-slice_fusion.2 = bf16[4,512,4096]{2,1,0:T(8,128)(2,1)} fusion(bf16[4,512,4096]{2,1,0:T(8,128)(2,1)} %get-tuple-element.60, s32[]{:T(128)S(6)} %copy.18, bf16[512,8192]{1,0:T(8,128)(2,1)} %get-tuple-element.63, s32[]{:T(128)} %bitcast.46), kind=kLoop, calls=%fused_computation.clone.1 | loop fusion | bytes 8389124 | tf_op jit(solution)/shard_map/vmap()/gather
  116.5 0.1 constant_dynamic-slice_fusion.2
  116.5 0.6 slice.40
  117.1 7.6 %bitcast_dynamic-update-slice_fusion.2 = bf16[4,512,4096]{2,1,0:T(8,128)(2,1)} fusion(bf16[4,512,4096]{2,1,0:T(8,128)(2,1)} %get-tuple-element.60, s32[]{:T(128)S(6)} %copy.18, bf16[512,8192]{1,0:T(8,128)(2,1)} %get-tuple-element.63, s32[]{:T(128)} %bitcast.46), kind=kLoop, calls=%fused_computation.clone.1 | loop fusion | bytes 8389124 | tf_op jit(solution)/shard_map/vmap()/gather
  124.7 0.1 constant_dynamic-slice_fusion.2
  124.8 0.6 slice.40
  125.4 7.6 %bitcast_dynamic-update-slice_fusion.2 = bf16[4,512,4096]{2,1,0:T(8,128)(2,1)} fusion(bf16[4,512,4096]{2,1,0:T(8,128)(2,1)} %get-tuple-element.60, s32[]{:T(128)S(6)} %copy.18, bf16[512,8192]{1,0:T(8,128)(2,1)} %get-tuple-element.63, s32[]{:T(128)} %bitcast.46), kind=kLoop, calls=%fused_computation.clone.1 | loop fusion | bytes 8389124 | tf_op jit(solution)/shard_map/vmap()/gather
  133.0 0.1 constant_dynamic-slice_fusion.2
  133.1 0.6 slice.40
  133.7 7.6 %bitcast_dynamic-update-slice_fusion.2 = bf16[4,512,4096]{2,1,0:T(8,128)(2,1)} fusion(bf16[4,512,4096]{2,1,0:T(8,128)(2,1)} %get-tuple-element.60, s32[]{:T(128)S(6)} %copy.18, bf16[512,8192]{1,0:T(8,128)(2,1)} %get-tuple-element.63, s32[]{:T(128)} %bitcast.46), kind=kLoop, calls=%fused_computation.clone.1 | loop fusion | bytes 8389124 | tf_op jit(solution)/shard_map/vmap()/gather
  141.3 8.8 %fusion.22 = bf16[4,2,128,512]{2,3,1,0:T(8,128)(2,1)S(1)} fusion(f32[1,128,4096]{2,1,0:T(8,128)} %get-tuple-element.26, f32[1,128,4096]{2,1,0:T(8,128)S(1)} %get-tuple-element.25, f32[4096]{0:T(1024)S(1)} %subtract_multiply_fusion, bf16[4,512,4096]{2,1,0:T(8,128)(2,1)} %get-tuple-element.12), kind=kOutput, calls=%fused_computation.28 | convolution fusion | flops 4298637312 | bytes 22036480 | tf_op jit(solution)/shard_map/tkn,scn->stkc/dot_general | solution.py:51
  150.1 2.0 copy.8
  152.1 4.0 %all-to-all-start = ((bf16[4,2,128,512]{3,1,0,2:T(2,128)(2,1)}), bf16[4,2,128,512]{3,1,0,2:T(2,128)(2,1)S(1)}, u32[]{:S(2)}, u32[]{:S(2)}) async-start(bf16[4,2,128,512]{3,1,0,2:T(2,128)(2,1)} %copy.8), calls=%async_computation | async-start | bytes 2097152 | tf_op jit(solution)/shard_map/all_to_all | solution.py:63
  156.1 24.9 %all-to-all-done = bf16[4,2,128,512]{3,1,0,2:T(2,128)(2,1)S(1)} async-done(((bf16[4,2,128,512]{3,1,0,2:T(2,128)(2,1)}), bf16[4,2,128,512]{3,1,0,2:T(2,128)(2,1)S(1)}, u32[]{:S(2)}, u32[]{:S(2)}) %all-to-all-start) | async-done | bytes 1048608 | tf_op jit(solution)/shard_map/all_to_all | solution.py:63
  181.0 0.3 copy.9
  181.3 0.8 copy.10
  182.2 0.3 all_to_all.16
  182.4 0.3 broadcast_in_dim.10
  182.7 0.9 fusion.34
  183.6 0.0 collective-permute-start.1
  183.6 1.7 collective-permute-start.2
  185.3 11.0 %collective-permute-done.1 = bf16[16,2,32,256]{3,0,1,2:T(8,128)(2,1)} collective-permute-done((bf16[16,2,32,256]{3,0,1,2:T(8,128)(2,1)}, bf16[16,2,32,256]{3,0,1,2:T(8,128)(2,1)}, u32[]{:S(2)}, u32[]{:S(2)}) %collective-permute-start.1) | collective-permute-done | bytes 524320 | tf_op jit(solution)/shard_map/ppermute | solution.py:16
  196.4 0.0 collective-permute-start.3
  196.4 1.1 constant_dynamic-update-slice_fusion.4
  197.5 0.0 collective-permute-done.2
  197.5 1.1 constant_dynamic-update-slice_fusion.3
  198.6 6.7 %collective-permute-done.3 = bf16[16,2,32,256]{3,0,1,2:T(8,128)(2,1)} collective-permute-done((bf16[16,2,32,256]{3,0,1,2:T(8,128)(2,1)}, bf16[16,2,32,256]{3,0,1,2:T(8,128)(2,1)}, u32[]{:S(2)}, u32[]{:S(2)}) %collective-permute-start.3) | collective-permute-done | bytes 524320 | tf_op jit(solution)/shard_map/ppermute | solution.py:16
  205.3 1.1 constant_dynamic-update-slice_fusion.2
  206.4 1.5 fusion.33
  207.9 8.1 %fusion = bf16[1,32,256,1024]{3,2,1,0:T(8,128)(2,1)} fusion(bf16[16,2,32,1024]{3,0,1,2:T(8,128)(2,1)S(1)} %constant_dynamic-update-slice_fusion.2, bf16[16,2,32,512]{3,0,1,2:T(8,128)(2,1)S(1)} %all_to_all.16), kind=kOutput, calls=%fused_computation.5 | convolution fusion | flops 545259520 | bytes 19398656 | tf_op jit(solution)/shard_map/gtkr,gtkp->krp/dot_general | solution.py:68
  216.0 9.6 %fusion.1 = bf16[1,32,256,1024]{3,2,1,0:T(8,128)(2,1)} fusion(bf16[16,1,32,1024]{3,0,1,2:T(8,128)(2,1)} %get-tuple-element.22, bf16[16,1,32,1024]{3,0,1,2:T(8,128)(2,1)} %get-tuple-element.21, bf16[16,2,32,512]{3,0,1,2:T(8,128)(2,1)S(1)} %all_to_all.16), kind=kOutput, calls=%fused_computation.6 | convolution fusion | flops 546308096 | bytes 19398656 | tf_op jit(solution)/shard_map/gtkr,gtkp->krp/dot_general | solution.py:71
  225.6 23.0 %pad_maximum_fusion = bf16[2,32,256,1024]{3,2,1,0:T(8,128)(2,1)} fusion(bf16[1,32,256,1024]{3,2,1,0:T(8,128)(2,1)} %fusion.1, bf16[1,32,256,1024]{3,2,1,0:T(8,128)(2,1)} %fusion), kind=kLoop, calls=%fused_computation.2 | loop fusion | flops 16777216 | bytes 67108864 | tf_op jit(solution)/shard_map/stack | solution.py:74
  (3 shorter events, 0.0 us)
Async XLA Ops:
  0.0 3.3 %copy-start = (bf16[256,4096]{1,0:T(8,128)(2,1)S(1)}, bf16[256,4096]{1,0:T(8,128)(2,1)}, u32[]{:S(2)}) copy-start(bf16[256,4096]{1,0:T(8,128)(2,1)} %param.5) | copy-start | bytes 6291460
  3.3 2.7 %copy-start.2 = (s32[4]{0:T(128)S(1)}, s32[4]{0:T(128)}, u32[]{:S(2)}) copy-start(s32[4]{0:T(128)} %param.6) | copy-start | bytes 52
  3.3 2.8 %copy-start.1 = (s32[128]{0:T(128)S(1)}, s32[128]{0:T(128)}, u32[]{:S(2)}) copy-start(s32[128]{0:T(128)} %param.7) | copy-start | bytes 1540
  4.7 95.8 %collective-permute-start = (bf16[512,4096]{1,0:T(8,128)(2,1)}, bf16[512,4096]{1,0:T(8,128)(2,1)}, u32[]{:S(2)}, u32[]{:S(2)}) collective-permute-start(bf16[512,4096]{1,0:T(8,128)(2,1)} %constant_dynamic-update-slice_fusion), channel_id=1, source_target_pairs={{4,0},{8,4},{12,8},{5,1},{9,5},{13,9},{6,2},{10,6},{14,10},{7,3},{... | collective-permute-start | bytes 12582920 | tf_op jit(solution)/shard_map/ppermute | solution.py:29
  152.1 28.9 %all-to-all-start = ((bf16[4,2,128,512]{3,1,0,2:T(2,128)(2,1)}), bf16[4,2,128,512]{3,1,0,2:T(2,128)(2,1)S(1)}, u32[]{:S(2)}, u32[]{:S(2)}) async-start(bf16[4,2,128,512]{3,1,0,2:T(2,128)(2,1)} %copy.8), calls=%async_computation | async-start | bytes 2097152 | tf_op jit(solution)/shard_map/all_to_all | solution.py:63
  183.6 12.8 %collective-permute-start.1 = (bf16[16,2,32,256]{3,0,1,2:T(8,128)(2,1)}, bf16[16,2,32,256]{3,0,1,2:T(8,128)(2,1)}, u32[]{:S(2)}, u32[]{:S(2)}) collective-permute-start(bf16[16,2,32,256]{3,0,1,2:T(8,128)(2,1)} %get-tuple-element.23), channel_id=1, source_target_pairs={{0,1},{1,2},{2,3},{3,0},{4,5},{5,6},{6,7},{7,4},{8,9},{9,10},{10,1... | collective-permute-start | bytes 1572872 | tf_op jit(solution)/shard_map/ppermute | solution.py:16
  183.6 13.9 %collective-permute-start.2 = (bf16[16,2,32,256]{3,0,1,2:T(8,128)(2,1)}, bf16[16,2,32,256]{3,0,1,2:T(8,128)(2,1)}, u32[]{:S(2)}, u32[]{:S(2)}) collective-permute-start(bf16[16,2,32,256]{3,0,1,2:T(8,128)(2,1)} %get-tuple-element.23), channel_id=1, source_target_pairs={{0,3},{1,0},{2,1},{3,2},{4,7},{5,4},{6,5},{7,6},{8,11},{9,8},{10,9... | collective-permute-start | bytes 1572872 | tf_op jit(solution)/shard_map/ppermute | solution.py:19
  196.4 8.9 %collective-permute-start.3 = (bf16[16,2,32,256]{3,0,1,2:T(8,128)(2,1)}, bf16[16,2,32,256]{3,0,1,2:T(8,128)(2,1)}, u32[]{:S(2)}, u32[]{:S(2)}) collective-permute-start(bf16[16,2,32,256]{3,0,1,2:T(8,128)(2,1)} %collective-permute-done.1), channel_id=1, source_target_pairs={{0,1},{1,2},{2,3},{3,0},{4,5},{5,6},{6,7},{7,4},{8,9},{9,10},{10,1... | collective-permute-start | bytes 1572872 | tf_op jit(solution)/shard_map/ppermute | solution.py:16
